TPU v7x, 512 devices: a whole 4x8x8 slice. The times are simulated.
512 devices in a mesh: row: 32 (over y, z_lo), col: 16 (over z_hi, x, core).
Axes of the slice: x: 4, y: 8, z: 8 (z_hi: 2, z_lo: 4; z = z_hi * 4 + z_lo), core: 2. Of those that a mesh axis runs over, the one named last changes fastest.
Arguments:
- embeddings: bfloat16 [8192, 256], P(('row', 'col')), may hold values from -6 to 6
- labels: bfloat16 [8192, 1024], P(('row', 'col')), may hold values from -6 to 6
- tile_mask: int32 [32, 32], replicated, may hold values 0 or 1
Outputs:
- spread_labels: bfloat16 [8192, 1024], P(('row', 'col'))
Inputs may be any that keep to these rules, and one draw needn't show every extreme that they name: Only the entries tile_mask[i, j] with i < j are read; the tile of blocks i and j (and of j and i) is kept where it is 1.
All inputs are finite; a program needn't handle non-finite values.
Results may differ from a plain program's by a relative error of at most 0.015.
Values may be sent and summed in bfloat16 or wider, within the bound.
A program may use at most 64 MiB of HBM per device.

v0:
```python
import math
import jax
import jax.numpy as jnp
from jax import lax
from jax.sharding import PartitionSpec as P

BLOCK = 256
ITERS = 2
MIXING = 0.9
SHARPNESS = 3.0
EPSILON = 1e-06


def unit_rows(embeddings):
    values = embeddings.astype(jnp.float32)
    return (values * lax.rsqrt(jnp.sum(values * values, axis=1, keepdims=True) + EPSILON)).astype(
        jnp.bfloat16
    )


def symmetric_keep(tile_mask):
    blocks = tile_mask.shape[0]
    block_row = lax.broadcasted_iota(jnp.int32, (blocks, blocks), 0)
    block_col = lax.broadcasted_iota(jnp.int32, (blocks, blocks), 1)
    mirrored = jnp.where(block_row < block_col, tile_mask, tile_mask.T)
    return (jnp.where(block_row == block_col, 1, mirrored), block_row, block_col)


def rotate_rows(values, start):
    total = values.shape[0]
    doubled = jnp.concatenate([values, values], axis=0)
    return lax.dynamic_slice_in_dim(doubled, start, total, 0)


def both_terms(operands):
    row_kernel, col_kernel, part_labels, row_labels = operands
    row_term = jnp.dot(row_kernel, part_labels, preferred_element_type=jnp.float32)
    col_term = lax.dot_general(
        col_kernel, row_labels, (((0,), (0,)), ((), ())), preferred_element_type=jnp.float32
    )
    return (row_term, col_term)


def no_terms(operands):
    row_kernel, col_kernel, part_labels, row_labels = operands
    return (
        jnp.zeros((row_kernel.shape[0], part_labels.shape[1]), jnp.float32),
        jnp.zeros((col_kernel.shape[1], row_labels.shape[1]), jnp.float32),
    )


def shards(embeddings, labels, tile_mask):
    row_count = lax.axis_size("row")
    col_count = lax.axis_size("col")
    row_index = lax.axis_index("row")
    col_index = lax.axis_index("col")
    piece_rows = embeddings.shape[0]
    emb_width = embeddings.shape[1]
    channels = labels.shape[1]
    blocks = tile_mask.shape[0]
    sharpness = SHARPNESS * math.sqrt(emb_width)
    unit_vecs = unit_rows(embeddings)
    row_units = lax.all_gather(unit_vecs, "col", axis=0, tiled=True)
    col_gathered = lax.all_gather(unit_vecs, "row", axis=0, tiled=True)
    row_total = row_units.shape[0]
    col_total = col_gathered.shape[0]
    shift = row_index * piece_rows
    back_shift = col_total - shift
    col_units = rotate_rows(col_gathered, shift)
    unit_count = math.gcd(8, row_count)
    unit_width = col_total // unit_count
    kept_sym, block_row, block_col = symmetric_keep(tile_mask)
    chosen = block_row <= block_col
    tile_table = jnp.where(chosen, kept_sym, 0)
    global_rows = row_index * row_total + jnp.arange(row_total, dtype=jnp.int32)
    row_blocks = global_rows // BLOCK
    block_ids = jnp.arange(blocks, dtype=jnp.int32)
    row_onehot = (row_blocks[:, None] == block_ids[None, :]).astype(jnp.bfloat16)
    row_table = jnp.dot(
        row_onehot, tile_table.astype(jnp.bfloat16), preferred_element_type=jnp.float32
    ).astype(jnp.bfloat16)
    local_cols = (jnp.arange(col_total, dtype=jnp.int32) + shift) % col_total
    global_cols = (
        local_cols // piece_rows * col_count + col_index
    ) * piece_rows + local_cols % piece_rows
    col_blocks = global_cols // BLOCK
    kernels_row = []
    kernels_col = []
    active_flags = []
    col_degree = []
    row_degree = jnp.zeros((row_total,), jnp.float32)
    for column_unit in range(unit_count):
        offset_cols = column_unit * unit_width
        part_units = col_units[offset_cols : offset_cols + unit_width]
        part_blocks = col_blocks[offset_cols : offset_cols + unit_width]
        part_cols = global_cols[offset_cols : offset_cols + unit_width]
        col_onehot = (part_blocks[:, None] == block_ids[None, :]).astype(jnp.bfloat16)
        kept_mask = lax.dot_general(
            row_table, col_onehot, (((1,), (1,)), ((), ())), preferred_element_type=jnp.float32
        )
        cosine = lax.dot_general(
            row_units, part_units, (((1,), (1,)), ((), ())), preferred_element_type=jnp.float32
        )
        distinct = global_rows[:, None] != part_cols[None, :]
        weights = jnp.where(
            distinct, jnp.exp(sharpness * cosine) * kept_mask, jnp.zeros_like(cosine)
        ).astype(jnp.bfloat16)
        active_flags.append(jnp.sum(kept_mask) > 0.0)
        kernels_row.append(weights)
        row_degree = row_degree + jnp.sum(weights, axis=1, dtype=jnp.float32)
        crossing = jnp.where(
            row_blocks[:, None] != part_blocks[None, :], weights, jnp.zeros_like(weights)
        )
        kernels_col.append(crossing)
        col_degree.append(jnp.sum(crossing, axis=0, dtype=jnp.float32))
    degree = lax.psum_scatter(row_degree, "col", scatter_dimension=0, tiled=True)
    col_sums = rotate_rows(jnp.concatenate(col_degree), back_shift)
    degree = degree + lax.psum_scatter(col_sums, "row", scatter_dimension=0, tiled=True)
    inv_root = lax.rsqrt(degree)
    seed_scores = labels.astype(jnp.float32)
    current = seed_scores
    for iteration in range(ITERS):
        scaled = (inv_root[:, None] * current).astype(jnp.bfloat16)
        col_labels = rotate_rows(lax.all_gather(scaled, "row", axis=0, tiled=True), shift)
        row_sum = jnp.zeros((row_total, channels), jnp.float32)
        col_parts = []
        row_labels = lax.all_gather(scaled, "col", axis=0, tiled=True)
        for column_unit in range(unit_count):
            offset_cols = column_unit * unit_width
            part_labels = col_labels[offset_cols : offset_cols + unit_width]
            row_term, col_term = lax.cond(
                active_flags[column_unit],
                both_terms,
                no_terms,
                (kernels_row[column_unit], kernels_col[column_unit], part_labels, row_labels),
            )
            row_sum = row_sum + row_term
            col_parts.append(col_term)
        sent_rows = row_sum.astype(jnp.bfloat16).reshape(col_count, piece_rows, channels)
        arrived = lax.all_to_all(sent_rows, "col", split_axis=0, concat_axis=0, tiled=True)
        spread = jnp.sum(arrived, axis=0, dtype=jnp.float32)
        ordered = rotate_rows(jnp.concatenate(col_parts).astype(jnp.bfloat16), back_shift)
        sent_cols = ordered.reshape(row_count, piece_rows, channels)
        returned = lax.all_to_all(sent_cols, "row", split_axis=0, concat_axis=0, tiled=True)
        spread = spread + jnp.sum(returned, axis=0, dtype=jnp.float32)
        current = MIXING * inv_root[:, None] * spread + (1.0 - MIXING) * seed_scores
    return current.astype(jnp.bfloat16)


def solution(mesh):
    placed = (P(("row", "col"), None), P(("row", "col"), None), P())
    return jax.shard_map(
        shards, mesh=mesh, in_specs=placed, out_specs=P(("row", "col"), None), check_vma=False
    )
```

profile of v0, /device:TPU:16, one launch (start us, length us, event | category | flops | bytes accessed | tf_op | source)
XLA Modules:
  0.0 721.4 jit_solution(1597081947624436445)
XLA Ops:
  8.1 35.3 %all_gather.18 = bf16[256,256]{1,0:T(8,128)(2,1)S(1)} all-gather(bf16[16,256]{1,0:T(8,128)(2,1)S(1)} %fusion.91), channel_id=1, replica_groups=mesh['row'=32,'col'=16] {'col'}, dimensions={0}, use_global_device_ids=true | all-gather | bytes 139264 | tf_op jit(solution)/shard_map/all_gather | solution.py:63
  43.4 67.6 %all_gather.19 = bf16[512,256]{1,0:T(8,128)(2,1)S(1)} all-gather(bf16[16,256]{1,0:T(8,128)(2,1)S(1)} %fusion.91), channel_id=1, replica_groups=mesh['row'=32,'col'=16] {'row'}, dimensions={0}, use_global_device_ids=true | all-gather | bytes 270336 | tf_op jit(solution)/shard_map/all_gather | solution.py:64
  111.0 1.3 dynamic-slice.2
  112.3 1.3 dynamic-slice
  115.8 1.0 convolution_convert_fusion.16
  125.5 1.2 convert_reduce_fusion.4
  126.9 73.2 %all-reduce.1 = f32[512]{0:T(512)S(1)} all-reduce(f32[512]{0:T(512)S(1)} %dynamic_slice.19), channel_id=3, replica_groups=mesh['row'=32,'col'=16] {'row'}, use_global_device_ids=true, to_apply=%region_18.19.clone | all-reduce | flops 512 | bytes 4096
  200.1 42.8 %all-reduce = f32[256]{0:T(256)S(1)} all-reduce(f32[256]{0:T(256)S(1)} %add_add_fusion), channel_id=2, replica_groups=mesh['row'=32,'col'=16] {'col'}, use_global_device_ids=true, to_apply=%region_9.10.clone | all-reduce | flops 256 | bytes 2048
  248.6 26.9 %all_gather.21 = bf16[256,1024]{1,0:T(8,128)(2,1)S(1)} all-gather(bf16[16,1024]{1,0:T(8,128)(2,1)} %fusion.72), channel_id=1, replica_groups=mesh['row'=32,'col'=16] {'col'}, dimensions={0}, use_global_device_ids=true | all-gather | bytes 557056 | tf_op jit(solution)/shard_map/all_gather | solution.py:127
  275.5 120.4 %all-gather.3.cloned.1.call-done = bf16[512,1024]{1,0:T(8,128)(2,1)} async-done(((bf16[16,1024]{1,0:T(8,128)(2,1)}), bf16[512,1024]{1,0:T(8,128)(2,1)}) %all-gather.3.cloned.1.call-update) | async-done | bytes 1048592 | tf_op jit(solution)/shard_map/all_gather | solution.py:124
  395.9 2.0 fusion.65
  398.0 1.3 conditional.16
  398.0 1.0 convolution_convert_fusion
  399.9 1.0 copy-done
  401.4 0.9 copy-done.1
  402.9 0.9 copy-done.2
  404.4 1.0 copy-done.3
  405.9 1.0 copy-done.4
  407.1 1.0 copy-done.5
  408.1 1.8 conditional.23
  408.7 1.1 broadcast.181
  409.8 4.7 add_convert_fusion.1
  414.5 7.0 all-to-all-start
  421.6 0.9 constant_dynamic-update-slice_fusion.8
  422.7 0.9 constant_dynamic-update-slice_fusion
  423.6 1.1 constant_dynamic-slice_fusion.1
  424.6 11.7 %all-to-all-done = bf16[16,16,1024]{2,1,0:T(8,128)(2,1)S(1)} async-done(((bf16[16,16,1024]{2,1,0:T(8,128)(2,1)}), bf16[16,16,1024]{2,1,0:T(8,128)(2,1)S(1)}, u32[]{:S(2)}, u32[]{:S(2)}) %all-to-all-start) | async-done | bytes 524320 | tf_op jit(solution)/shard_map/all_to_all | solution.py:140
  436.3 17.4 %all-to-all-start.1 = ((bf16[32,16,1024]{2,1,0:T(8,128)(2,1)}), bf16[32,16,1024]{2,1,0:T(8,128)(2,1)S(1)}, u32[]{:S(2)}, u32[]{:S(2)}) async-start(bf16[32,16,1024]{2,1,0:T(8,128)(2,1)} %bitcast.2), calls=%async_computation.1 | async-start | bytes 2097152 | tf_op jit(solution)/shard_map/all_to_all | solution.py:144
  453.9 28.7 %all-to-all-done.1 = bf16[32,16,1024]{2,1,0:T(8,128)(2,1)S(1)} async-done(((bf16[32,16,1024]{2,1,0:T(8,128)(2,1)}), bf16[32,16,1024]{2,1,0:T(8,128)(2,1)S(1)}, u32[]{:S(2)}, u32[]{:S(2)}) %all-to-all-start.1) | async-done | bytes 1048608 | tf_op jit(solution)/shard_map/all_to_all | solution.py:144
  483.5 32.2 %all_gather.23 = bf16[256,1024]{1,0:T(8,128)(2,1)S(1)} all-gather(bf16[16,1024]{1,0:T(8,128)(2,1)} %fusion.70), channel_id=1, replica_groups=mesh['row'=32,'col'=16] {'col'}, dimensions={0}, use_global_device_ids=true | all-gather | bytes 557056 | tf_op jit(solution)/shard_map/all_gather | solution.py:127
  515.7 110.3 %all-gather.5.cloned.1.call-done = bf16[512,1024]{1,0:T(8,128)(2,1)} async-done(((bf16[16,1024]{1,0:T(8,128)(2,1)}), bf16[512,1024]{1,0:T(8,128)(2,1)}) %all-gather.5.cloned.1.call-update) | async-done | bytes 1048592 | tf_op jit(solution)/shard_map/all_gather | solution.py:124
  626.0 2.0 fusion.64
  628.0 1.3 conditional.24
  628.0 1.0 convolution_convert_fusion.8
  630.7 0.9 copy-done.6
  632.2 1.0 copy-done.7
  633.8 1.0 copy-done.8
  635.3 1.0 copy-done.9
  636.8 1.0 copy-done.10
  637.9 1.0 copy-done.11
  638.9 1.8 conditional.31
  639.6 1.1 broadcast.197
  640.7 4.7 add_convert_fusion
  645.3 7.3 %all-to-all-start.2 = ((bf16[16,16,1024]{2,1,0:T(8,128)(2,1)}), bf16[16,16,1024]{2,1,0:T(8,128)(2,1)S(1)}, u32[]{:S(2)}, u32[]{:S(2)}) async-start(bf16[16,16,1024]{2,1,0:T(8,128)(2,1)} %bitcast.3), calls=%async_computation.2 | async-start | bytes 1048576 | tf_op jit(solution)/shard_map/all_to_all | solution.py:140
  654.7 1.1 constant_dynamic-slice_fusion
  655.8 11.7 %all-to-all-done.2 = bf16[16,16,1024]{2,1,0:T(8,128)(2,1)S(1)} async-done(((bf16[16,16,1024]{2,1,0:T(8,128)(2,1)}), bf16[16,16,1024]{2,1,0:T(8,128)(2,1)S(1)}, u32[]{:S(2)}, u32[]{:S(2)}) %all-to-all-start.2) | async-done | bytes 524320 | tf_op jit(solution)/shard_map/all_to_all | solution.py:140
  667.5 17.4 %all-to-all-start.3 = ((bf16[32,16,1024]{2,1,0:T(8,128)(2,1)}), bf16[32,16,1024]{2,1,0:T(8,128)(2,1)S(1)}, u32[]{:S(2)}, u32[]{:S(2)}) async-start(bf16[32,16,1024]{2,1,0:T(8,128)(2,1)} %bitcast.4), calls=%async_computation.3 | async-start | bytes 2097152 | tf_op jit(solution)/shard_map/all_to_all | solution.py:144
  684.9 28.8 %all-to-all-done.3 = bf16[32,16,1024]{2,1,0:T(8,128)(2,1)S(1)} async-done(((bf16[32,16,1024]{2,1,0:T(8,128)(2,1)}), bf16[32,16,1024]{2,1,0:T(8,128)(2,1)S(1)}, u32[]{:S(2)}, u32[]{:S(2)}) %all-to-all-start.3) | async-done | bytes 1048608 | tf_op jit(solution)/shard_map/all_to_all | solution.py:144
  (173 shorter events, 30.1 us)
Async XLA Ops:
  6.5 389.4 %all-gather.3.cloned.1.call-start = ((), (), s32[]{:S(2)}) async-start(), calls=%async_computation.4 | async-start | bytes 1081344 | tf_op jit(solution)/shard_map/all_gather | solution.py:124
  118.4 124.5 %copy-start.25 = (bf16[16,1024]{1,0:T(8,128)(2,1)S(1)}, bf16[16,1024]{1,0:T(8,128)(2,1)}, u32[]{:S(2)}) copy-start(bf16[16,1024]{1,0:T(8,128)(2,1)} %param.36) | copy-start | bytes 98308
  124.2 2.5 copy-start.12
  124.4 280.0 %copy-start.13 = (bf16[256,64]{0,1:T(8,128)(2,1)}, bf16[256,64]{0,1:T(8,128)(2,1)S(1)}, u32[]{:S(2)}) copy-start(bf16[256,64]{0,1:T(8,128)(2,1)S(1)} %fusion.58) | copy-start | bytes 98308
  124.6 278.3 %copy-start.15 = (bf16[256,64]{0,1:T(8,128)(2,1)}, bf16[256,64]{0,1:T(8,128)(2,1)S(1)}, u32[]{:S(2)}) copy-start(bf16[256,64]{0,1:T(8,128)(2,1)S(1)} %fusion.59) | copy-start | bytes 98308
  124.9 276.5 %copy-start.17 = (bf16[256,64]{0,1:T(8,128)(2,1)}, bf16[256,64]{0,1:T(8,128)(2,1)S(1)}, u32[]{:S(2)}) copy-start(bf16[256,64]{0,1:T(8,128)(2,1)S(1)} %fusion.60) | copy-start | bytes 98308
  125.1 274.8 %copy-start.19 = (bf16[256,64]{0,1:T(8,128)(2,1)}, bf16[256,64]{0,1:T(8,128)(2,1)S(1)}, u32[]{:S(2)}) copy-start(bf16[256,64]{0,1:T(8,128)(2,1)S(1)} %fusion.61) | copy-start | bytes 98308
  125.3 274.0 %copy-start.21 = (bf16[256,64]{0,1:T(8,128)(2,1)}, bf16[256,64]{0,1:T(8,128)(2,1)S(1)}, u32[]{:S(2)}) copy-start(bf16[256,64]{0,1:T(8,128)(2,1)S(1)} %fusion.62) | copy-start | bytes 98308
  125.5 272.4 %copy-start.23 = (bf16[256,64]{0,1:T(8,128)(2,1)}, bf16[256,64]{0,1:T(8,128)(2,1)S(1)}, u32[]{:S(2)}) copy-start(bf16[256,64]{0,1:T(8,128)(2,1)S(1)} %fusion.63) | copy-start | bytes 98308
  126.7 272.6 %copy-start.36 = (bf16[256,64]{0,1:T(8,128)(2,1)}, bf16[256,64]{0,1:T(8,128)(2,1)S(1)}, u32[]{:S(2)}) copy-start(bf16[256,64]{0,1:T(8,128)(2,1)S(1)} %get-tuple-element.465) | copy-start | bytes 98308
  126.7 273.2 %copy-start.34 = (bf16[256,64]{0,1:T(8,128)(2,1)}, bf16[256,64]{0,1:T(8,128)(2,1)S(1)}, u32[]{:S(2)}) copy-start(bf16[256,64]{0,1:T(8,128)(2,1)S(1)} %get-tuple-element.468) | copy-start | bytes 98308
  126.7 274.7 %copy-start.32 = (bf16[256,64]{0,1:T(8,128)(2,1)}, bf16[256,64]{0,1:T(8,128)(2,1)S(1)}, u32[]{:S(2)}) copy-start(bf16[256,64]{0,1:T(8,128)(2,1)S(1)} %get-tuple-element.471) | copy-start | bytes 98308
  126.7 276.2 %copy-start.30 = (bf16[256,64]{0,1:T(8,128)(2,1)}, bf16[256,64]{0,1:T(8,128)(2,1)S(1)}, u32[]{:S(2)}) copy-start(bf16[256,64]{0,1:T(8,128)(2,1)S(1)} %get-tuple-element.474) | copy-start | bytes 98308
  126.7 277.7 %copy-start.28 = (bf16[256,64]{0,1:T(8,128)(2,1)}, bf16[256,64]{0,1:T(8,128)(2,1)S(1)}, u32[]{:S(2)}) copy-start(bf16[256,64]{0,1:T(8,128)(2,1)S(1)} %get-tuple-element.477) | copy-start | bytes 98308
  399.8 1.0 copy-start
  401.4 1.0 copy-start.1
  402.9 1.0 copy-start.2
  404.4 1.0 copy-start.3
  405.9 1.0 copy-start.4
  407.1 1.0 copy-start.5
  414.5 21.8 %all-to-all-start = ((bf16[16,16,1024]{2,1,0:T(8,128)(2,1)}), bf16[16,16,1024]{2,1,0:T(8,128)(2,1)S(1)}, u32[]{:S(2)}, u32[]{:S(2)}) async-start(bf16[16,16,1024]{2,1,0:T(8,128)(2,1)} %bitcast.1), calls=%async_computation | async-start | bytes 1048576 | tf_op jit(solution)/shard_map/all_to_all | solution.py:140
  424.6 58.1 %copy-start.26 = (bf16[16,1024]{1,0:T(8,128)(2,1)S(1)}, bf16[16,1024]{1,0:T(8,128)(2,1)}, u32[]{:S(2)}) copy-start(bf16[16,1024]{1,0:T(8,128)(2,1)} %param.36) | copy-start | bytes 98308
  436.3 46.3 %all-to-all-start.1 = ((bf16[32,16,1024]{2,1,0:T(8,128)(2,1)}), bf16[32,16,1024]{2,1,0:T(8,128)(2,1)S(1)}, u32[]{:S(2)}, u32[]{:S(2)}) async-start(bf16[32,16,1024]{2,1,0:T(8,128)(2,1)} %bitcast.2), calls=%async_computation.1 | async-start | bytes 2097152 | tf_op jit(solution)/shard_map/all_to_all | solution.py:144
  453.7 172.3 %all-gather.5.cloned.1.call-start = ((), (), s32[]{:S(2)}) async-start(), calls=%async_computation.5 | async-start | bytes 1081344 | tf_op jit(solution)/shard_map/all_gather | solution.py:124
  453.9 174.1 %copy-start.24 = (bf16[256,64]{0,1:T(8,128)(2,1)S(1)}, bf16[256,64]{0,1:T(8,128)(2,1)}, u32[]{:S(2)}) copy-start(bf16[256,64]{0,1:T(8,128)(2,1)} %copy-done.23) | copy-start | bytes 98308
  515.7 112.3 %copy-start.22 = (bf16[256,64]{0,1:T(8,128)(2,1)S(1)}, bf16[256,64]{0,1:T(8,128)(2,1)}, u32[]{:S(2)}) copy-start(bf16[256,64]{0,1:T(8,128)(2,1)} %copy-done.21) | copy-start | bytes 98308
  515.7 112.3 %copy-start.37 = (bf16[256,64]{0,1:T(8,128)(2,1)S(1)}, bf16[256,64]{0,1:T(8,128)(2,1)}, u32[]{:S(2)}) copy-start(bf16[256,64]{0,1:T(8,128)(2,1)} %copy-done.36) | copy-start | bytes 98308
  629.3 0.8 copy-start.20
  629.4 0.8 copy-start.35
  630.7 1.0 copy-start.6
  630.7 1.0 copy-start.18
  630.7 1.0 copy-start.33
  632.2 1.0 copy-start.7
  632.2 1.0 copy-start.16
  632.2 1.0 copy-start.31
  633.7 1.0 copy-start.8
  633.7 1.0 copy-start.14
  633.8 1.0 copy-start.29
  635.3 1.0 copy-start.9
  636.8 1.0 copy-start.10
  637.9 1.0 copy-start.11
  645.3 22.1 %all-to-all-start.2 = ((bf16[16,16,1024]{2,1,0:T(8,128)(2,1)}), bf16[16,16,1024]{2,1,0:T(8,128)(2,1)S(1)}, u32[]{:S(2)}, u32[]{:S(2)}) async-start(bf16[16,16,1024]{2,1,0:T(8,128)(2,1)} %bitcast.3), calls=%async_computation.2 | async-start | bytes 1048576 | tf_op jit(solution)/shard_map/all_to_all | solution.py:140
  655.8 58.1 %copy-start.27 = (bf16[16,1024]{1,0:T(8,128)(2,1)S(1)}, bf16[16,1024]{1,0:T(8,128)(2,1)}, u32[]{:S(2)}) copy-start(bf16[16,1024]{1,0:T(8,128)(2,1)} %param.36) | copy-start | bytes 98308
  667.5 46.2 %all-to-all-start.3 = ((bf16[32,16,1024]{2,1,0:T(8,128)(2,1)}), bf16[32,16,1024]{2,1,0:T(8,128)(2,1)S(1)}, u32[]{:S(2)}, u32[]{:S(2)}) async-start(bf16[32,16,1024]{2,1,0:T(8,128)(2,1)} %bitcast.4), calls=%async_computation.3 | async-start | bytes 2097152 | tf_op jit(solution)/shard_map/all_to_all | solution.py:144
Sparse Core Ops, SparseCore 0:
  243.8 152.1 all-gather.2
  483.6 142.3 all-gather.4
where the time goes:
time: 723 us; the launch traced here: 721 us
  waiting for transfers between devices  312 us (43%)
  blocking collectives  278 us (38%)
  starting transfers between devices  49.1 us (7%)
  local copies, waits for them, and re-layouts  26 us (4%)
  between operations  20.4 us (3%)
  other arithmetic  18.2 us (3%)
  matrix products  17.9 us (2%)
    all_gather x2, waiting for transfers between devices, shards(): lax.all_gather(scaled, 'row', axis=0, tiled=True)  231 us
    unnamed x2, blocking collectives  116 us
    all_gather x1, blocking collectives, shards(): col_gathered = lax.all_gather(unit_vecs, 'row', axis=0, tiled=True)  67.6 us
    all_gather x2, blocking collectives, shards(): row_labels = lax.all_gather(scaled, 'col', axis=0, tiled=True)  59.1 us
    all_to_all x2, waiting for transfers between devices, shards(): lax.all_to_all(sent_cols, 'row', split_axis=0, concat_axis=0, tiled=True)  57.5 us
    all_gather x1, blocking collectives, shards(): row_units = lax.all_gather(unit_vecs, 'col', axis=0, tiled=True)  35.3 us
    all_to_all x2, starting transfers between devices, shards(): lax.all_to_all(sent_cols, 'row', split_axis=0, concat_axis=0, tiled=True)  34.8 us
    all_to_all x2, waiting for transfers between devices, shards(): lax.all_to_all(sent_rows, 'col', split_axis=0, concat_axis=0, tiled=True)  23.4 us
  transfers between devices with their start and end apart: 6, of which 6 were waited for; matrix products, arithmetic and copies ran while one was open for 1% of the time, Pallas kernels for 0%

commit v1 on v0

--- a/solution.py
+++ b/solution.py
@@ -121,7 +121,12 @@
     current = seed_scores
     for iteration in range(ITERS):
         scaled = (inv_root[:, None] * current).astype(jnp.bfloat16)
-        col_labels = rotate_rows(lax.all_gather(scaled, "row", axis=0, tiled=True), shift)
+        col_labels = rotate_rows(
+            jnp.concatenate(
+                lax.all_to_all(jnp.stack([scaled] * lax.axis_size("row")), "row", 0, 0), axis=0
+            ),
+            shift,
+        )
         row_sum = jnp.zeros((row_total, channels), jnp.float32)
         col_parts = []
         row_labels = lax.all_gather(scaled, "col", axis=0, tiled=True)

time: 723 us -> 506 us (0.70)
  waiting for transfers between devices: 312 us -> 79.2 us
  blocking collectives: 278 us -> 303 us
  between operations: 20.4 us -> 7.16 us
    all_gather x2 -> x0, waiting for transfers between devices: 231 us -> none  [shards(): lax.all_gather(scaled, 'row', axis=0, tiled=True)]
    all_gather x2, blocking collectives: 59.1 us -> 84.5 us  [shards(): row_labels = lax.all_gather(scaled, 'col', axis=0, tiled=True)]
    all_to_all x0 -> x2, starting transfers between devices: none -> 24.6 us  [shards(): lax.all_to_all(jnp.stack([scaled] * lax.axis_size('row')), 'row', 0, 0)]
    all_to_all x2, starting transfers between devices: 34.8 us -> 19 us  [shards(): lax.all_to_all(sent_cols, 'row', split_axis=0, concat_axis=0, tiled=True)]
    unnamed x109 -> x115, local copies, waits for them, and re-layouts: 18 us -> 20 us
  transfers between devices with their start and end apart: 6 -> 6, of which waited for: 6 -> 4; matrix products, arithmetic and copies ran while one was open for 1% -> 1% of each run, Pallas kernels for 0% -> 0%
where the time goes in v1:
time: 506 us; the launch traced here: 504 us
  blocking collectives  303 us (60%)
  waiting for transfers between devices  79.2 us (16%)
  starting transfers between devices  50.8 us (10%)
  local copies, waits for them, and re-layouts  28.4 us (6%)
  matrix products  19.3 us (4%)
  other arithmetic  15.6 us (3%)
  between operations  7.16 us (1%)
    unnamed x2, blocking collectives  116 us
    all_gather x2, blocking collectives, shards(): row_labels = lax.all_gather(scaled, 'col', axis=0, tiled=True)  84.5 us
    all_gather x1, blocking collectives, shards(): col_gathered = lax.all_gather(unit_vecs, 'row', axis=0, tiled=True)  67.6 us
    all_to_all x2, waiting for transfers between devices, shards(): lax.all_to_all(sent_cols, 'row', split_axis=0, concat_axis=0, tiled=True)  56.1 us
    all_gather x1, blocking collectives, shards(): row_units = lax.all_gather(unit_vecs, 'col', axis=0, tiled=True)  35.3 us
    all_to_all x2, starting transfers between devices, shards(): lax.all_to_all(jnp.stack([scaled] * lax.axis_size('row')), 'row', 0, 0)  24.6 us
    all_to_all x2, waiting for transfers between devices, shards(): lax.all_to_all(sent_rows, 'col', split_axis=0, concat_axis=0, tiled=True)  23.1 us
    unnamed x115, local copies, waits for them, and re-layouts  20 us
  transfers between devices with their start and end apart: 6, of which 4 were waited for; matrix products, arithmetic and copies ran while one was open for 1% of the time, Pallas kernels for 0%

profile of v1, /device:TPU:16, one launch (start us, length us, event | category | flops | bytes accessed | tf_op | source)
XLA Modules:
  0.0 504.1 jit_solution(16850610361621237555)
XLA Ops:
  1.6 35.3 %all_gather.12 = bf16[256,256]{1,0:T(8,128)(2,1)S(1)} all-gather(bf16[16,256]{1,0:T(8,128)(2,1)S(1)} %fusion.91), channel_id=1, replica_groups=mesh['row'=32,'col'=16] {'col'}, dimensions={0}, use_global_device_ids=true | all-gather | bytes 139264 | tf_op jit(solution)/shard_map/all_gather | solution.py:63
  36.9 67.6 %all_gather.13 = bf16[512,256]{1,0:T(8,128)(2,1)S(1)} all-gather(bf16[16,256]{1,0:T(8,128)(2,1)S(1)} %fusion.91), channel_id=1, replica_groups=mesh['row'=32,'col'=16] {'row'}, dimensions={0}, use_global_device_ids=true | all-gather | bytes 270336 | tf_op jit(solution)/shard_map/all_gather | solution.py:64
  104.5 1.3 dynamic-slice.2
  105.8 1.3 dynamic-slice
  109.4 1.0 convolution_convert_fusion.16
  119.2 1.1 convert_reduce_fusion.4
  120.5 73.2 %all-reduce.1 = f32[512]{0:T(512)S(1)} all-reduce(f32[512]{0:T(512)S(1)} %dynamic_slice.19), channel_id=3, replica_groups=mesh['row'=32,'col'=16] {'row'}, use_global_device_ids=true, to_apply=%region_18.19.clone | all-reduce | flops 512 | bytes 4096
  193.6 42.8 %all-reduce = f32[256]{0:T(256)S(1)} all-reduce(f32[256]{0:T(256)S(1)} %add_add_fusion), channel_id=2, replica_groups=mesh['row'=32,'col'=16] {'col'}, use_global_device_ids=true, to_apply=%region_9.10.clone | all-reduce | flops 256 | bytes 2048
  236.6 1.1 stack.4
  237.7 19.9 %all-to-all-start = ((bf16[32,16,1024]{2,1,0:T(8,128)(2,1)}), bf16[32,16,1024]{2,1,0:T(8,128)(2,1)S(1)}, u32[]{:S(2)}, u32[]{:S(2)}) async-start(bf16[32,16,1024]{2,1,0:T(8,128)(2,1)} %stack.4), calls=%async_computation | async-start | bytes 2097152 | tf_op jit(solution)/shard_map/all_to_all | solution.py:126
  262.5 39.2 %all_gather.14 = bf16[256,1024]{1,0:T(8,128)(2,1)S(1)} all-gather(bf16[16,1024]{1,0:T(8,128)(2,1)S(1)} %fusion.72), channel_id=1, replica_groups=mesh['row'=32,'col'=16] {'col'}, dimensions={0}, use_global_device_ids=true | all-gather | bytes 557056 | tf_op jit(solution)/shard_map/all_gather | solution.py:132
  301.7 1.3 fusion.65
  305.3 1.0 copy-done.1
  306.8 1.0 copy-done.2
  308.3 1.0 copy-done.3
  309.9 1.0 copy-done.4
  310.9 2.0 conditional.21
  310.9 1.0 convolution_convert_fusion.5
  311.9 1.1 fusion.10
  312.9 1.0 copy-done.5
  313.9 1.8 conditional.22
  314.6 1.1 broadcast.183
  315.7 4.7 add_convert_fusion.1
  320.4 3.6 all-to-all-start.1
  326.1 1.0 constant_dynamic-slice_fusion.1
  327.1 11.6 %all-to-all-done.1 = bf16[16,16,1024]{2,1,0:T(8,128)(2,1)S(1)} async-done(((bf16[16,16,1024]{2,1,0:T(8,128)(2,1)}), bf16[16,16,1024]{2,1,0:T(8,128)(2,1)S(1)}, u32[]{:S(2)}, u32[]{:S(2)}) %all-to-all-start.1) | async-done | bytes 524320 | tf_op jit(solution)/shard_map/all_to_all | solution.py:145
  338.7 10.2 %all-to-all-start.2 = ((bf16[32,16,1024]{2,1,0:T(8,128)(2,1)}), bf16[32,16,1024]{2,1,0:T(8,128)(2,1)S(1)}, u32[]{:S(2)}, u32[]{:S(2)}) async-start(bf16[32,16,1024]{2,1,0:T(8,128)(2,1)} %bitcast.3), calls=%async_computation.2 | async-start | bytes 2097152 | tf_op jit(solution)/shard_map/all_to_all | solution.py:149
  349.0 28.1 %all-to-all-done.2 = bf16[32,16,1024]{2,1,0:T(8,128)(2,1)S(1)} async-done(((bf16[32,16,1024]{2,1,0:T(8,128)(2,1)}), bf16[32,16,1024]{2,1,0:T(8,128)(2,1)S(1)}, u32[]{:S(2)}, u32[]{:S(2)}) %all-to-all-start.2) | async-done | bytes 1048608 | tf_op jit(solution)/shard_map/all_to_all | solution.py:149
  377.3 1.1 stack.5
  378.4 4.7 all-to-all-start.3
  383.2 45.4 %all_gather.15 = bf16[256,1024]{1,0:T(8,128)(2,1)S(1)} all-gather(bf16[16,1024]{1,0:T(8,128)(2,1)S(1)} %fusion.70), channel_id=1, replica_groups=mesh['row'=32,'col'=16] {'col'}, dimensions={0}, use_global_device_ids=true | all-gather | bytes 557056 | tf_op jit(solution)/shard_map/all_gather | solution.py:132
  428.6 1.3 fusion.64
  432.9 1.0 copy-done.7
  434.5 1.0 copy-done.8
  436.0 1.0 copy-done.9
  437.5 1.0 copy-done.10
  438.5 2.0 conditional.29
  438.5 1.0 convolution_convert_fusion.13
  439.5 1.1 fusion.26
  440.6 1.0 copy-done.11
  441.5 1.8 conditional.30
  442.2 1.1 broadcast.199
  443.3 4.7 add_convert_fusion
  448.0 3.6 all-to-all-start.4
  453.7 1.0 constant_dynamic-slice_fusion
  454.8 11.6 %all-to-all-done.4 = bf16[16,16,1024]{2,1,0:T(8,128)(2,1)S(1)} async-done(((bf16[16,16,1024]{2,1,0:T(8,128)(2,1)}), bf16[16,16,1024]{2,1,0:T(8,128)(2,1)S(1)}, u32[]{:S(2)}, u32[]{:S(2)}) %all-to-all-start.4) | async-done | bytes 524320 | tf_op jit(solution)/shard_map/all_to_all | solution.py:145
  466.3 8.7 %all-to-all-start.5 = ((bf16[32,16,1024]{2,1,0:T(8,128)(2,1)}), bf16[32,16,1024]{2,1,0:T(8,128)(2,1)S(1)}, u32[]{:S(2)}, u32[]{:S(2)}) async-start(bf16[32,16,1024]{2,1,0:T(8,128)(2,1)} %bitcast.6), calls=%async_computation.5 | async-start | bytes 2097152 | tf_op jit(solution)/shard_map/all_to_all | solution.py:149
  475.1 28.1 %all-to-all-done.5 = bf16[32,16,1024]{2,1,0:T(8,128)(2,1)S(1)} async-done(((bf16[32,16,1024]{2,1,0:T(8,128)(2,1)}), bf16[32,16,1024]{2,1,0:T(8,128)(2,1)S(1)}, u32[]{:S(2)}, u32[]{:S(2)}) %all-to-all-start.5) | async-done | bytes 1048608 | tf_op jit(solution)/shard_map/all_to_all | solution.py:149
  (179 shorter events, 32.0 us)
Async XLA Ops:
  112.1 124.4 %copy-start.24 = (bf16[16,1024]{1,0:T(8,128)(2,1)S(1)}, bf16[16,1024]{1,0:T(8,128)(2,1)}, u32[]{:S(2)}) copy-start(bf16[16,1024]{1,0:T(8,128)(2,1)} %param.36) | copy-start | bytes 98308
  117.8 119.8 %copy-start.12 = (bf16[256,64]{0,1:T(8,128)(2,1)}, bf16[256,64]{0,1:T(8,128)(2,1)S(1)}, u32[]{:S(2)}) copy-start(bf16[256,64]{0,1:T(8,128)(2,1)S(1)} %fusion.57) | copy-start | bytes 98308
  118.1 119.6 %copy-start.13 = (bf16[256,64]{0,1:T(8,128)(2,1)}, bf16[256,64]{0,1:T(8,128)(2,1)S(1)}, u32[]{:S(2)}) copy-start(bf16[256,64]{0,1:T(8,128)(2,1)S(1)} %fusion.58) | copy-start | bytes 98308
  118.3 190.0 %copy-start.14 = (bf16[256,64]{0,1:T(8,128)(2,1)}, bf16[256,64]{0,1:T(8,128)(2,1)S(1)}, u32[]{:S(2)}) copy-start(bf16[256,64]{0,1:T(8,128)(2,1)S(1)} %fusion.59) | copy-start | bytes 98308
  118.5 188.3 %copy-start.16 = (bf16[256,64]{0,1:T(8,128)(2,1)}, bf16[256,64]{0,1:T(8,128)(2,1)S(1)}, u32[]{:S(2)}) copy-start(bf16[256,64]{0,1:T(8,128)(2,1)S(1)} %fusion.60) | copy-start | bytes 98308
  118.7 186.5 %copy-start.18 = (bf16[256,64]{0,1:T(8,128)(2,1)}, bf16[256,64]{0,1:T(8,128)(2,1)S(1)}, u32[]{:S(2)}) copy-start(bf16[256,64]{0,1:T(8,128)(2,1)S(1)} %fusion.61) | copy-start | bytes 98308
  118.9 184.8 %copy-start.20 = (bf16[256,64]{0,1:T(8,128)(2,1)}, bf16[256,64]{0,1:T(8,128)(2,1)S(1)}, u32[]{:S(2)}) copy-start(bf16[256,64]{0,1:T(8,128)(2,1)S(1)} %fusion.62) | copy-start | bytes 98308
  119.1 184.0 %copy-start.22 = (bf16[256,64]{0,1:T(8,128)(2,1)}, bf16[256,64]{0,1:T(8,128)(2,1)S(1)}, u32[]{:S(2)}) copy-start(bf16[256,64]{0,1:T(8,128)(2,1)S(1)} %fusion.63) | copy-start | bytes 98308
  120.2 182.8 %copy-start.27 = (bf16[256,64]{0,1:T(8,128)(2,1)}, bf16[256,64]{0,1:T(8,128)(2,1)S(1)}, u32[]{:S(2)}) copy-start(bf16[256,64]{0,1:T(8,128)(2,1)S(1)} %get-tuple-element.486) | copy-start | bytes 98308
  120.2 182.8 %copy-start.39 = (bf16[256,64]{0,1:T(8,128)(2,1)}, bf16[256,64]{0,1:T(8,128)(2,1)S(1)}, u32[]{:S(2)}) copy-start(bf16[256,64]{0,1:T(8,128)(2,1)S(1)} %get-tuple-element.424) | copy-start | bytes 98308
  120.3 182.9 %copy-start.37 = (bf16[256,64]{0,1:T(8,128)(2,1)}, bf16[256,64]{0,1:T(8,128)(2,1)S(1)}, u32[]{:S(2)}) copy-start(bf16[256,64]{0,1:T(8,128)(2,1)S(1)} %get-tuple-element.483) | copy-start | bytes 98308
  120.3 183.5 %copy-start.35 = (bf16[256,64]{0,1:T(8,128)(2,1)}, bf16[256,64]{0,1:T(8,128)(2,1)S(1)}, u32[]{:S(2)}) copy-start(bf16[256,64]{0,1:T(8,128)(2,1)S(1)} %get-tuple-element.465) | copy-start | bytes 98308
  120.3 185.0 %copy-start.33 = (bf16[256,64]{0,1:T(8,128)(2,1)}, bf16[256,64]{0,1:T(8,128)(2,1)S(1)}, u32[]{:S(2)}) copy-start(bf16[256,64]{0,1:T(8,128)(2,1)S(1)} %get-tuple-element.468) | copy-start | bytes 98308
  120.3 186.5 %copy-start.31 = (bf16[256,64]{0,1:T(8,128)(2,1)}, bf16[256,64]{0,1:T(8,128)(2,1)S(1)}, u32[]{:S(2)}) copy-start(bf16[256,64]{0,1:T(8,128)(2,1)S(1)} %get-tuple-element.471) | copy-start | bytes 98308
  120.3 188.0 %copy-start.29 = (bf16[256,64]{0,1:T(8,128)(2,1)}, bf16[256,64]{0,1:T(8,128)(2,1)S(1)}, u32[]{:S(2)}) copy-start(bf16[256,64]{0,1:T(8,128)(2,1)S(1)} %get-tuple-element.474) | copy-start | bytes 98308
  237.7 64.0 %all-to-all-start = ((bf16[32,16,1024]{2,1,0:T(8,128)(2,1)}), bf16[32,16,1024]{2,1,0:T(8,128)(2,1)S(1)}, u32[]{:S(2)}, u32[]{:S(2)}) async-start(bf16[32,16,1024]{2,1,0:T(8,128)(2,1)} %stack.4), calls=%async_computation | async-start | bytes 2097152 | tf_op jit(solution)/shard_map/all_to_all | solution.py:126
  303.7 1.0 copy-start
  305.2 1.0 copy-start.1
  306.8 1.0 copy-start.2
  308.3 1.0 copy-start.3
  309.8 1.0 copy-start.4
  312.9 1.0 copy-start.5
  320.4 18.3 %all-to-all-start.1 = ((bf16[16,16,1024]{2,1,0:T(8,128)(2,1)}), bf16[16,16,1024]{2,1,0:T(8,128)(2,1)S(1)}, u32[]{:S(2)}, u32[]{:S(2)}) async-start(bf16[16,16,1024]{2,1,0:T(8,128)(2,1)} %bitcast.2), calls=%async_computation.1 | async-start | bytes 1048576 | tf_op jit(solution)/shard_map/all_to_all | solution.py:145
  327.1 50.1 %copy-start.25 = (bf16[16,1024]{1,0:T(8,128)(2,1)S(1)}, bf16[16,1024]{1,0:T(8,128)(2,1)}, u32[]{:S(2)}) copy-start(bf16[16,1024]{1,0:T(8,128)(2,1)} %param.36) | copy-start | bytes 98308
  338.7 38.4 %all-to-all-start.2 = ((bf16[32,16,1024]{2,1,0:T(8,128)(2,1)}), bf16[32,16,1024]{2,1,0:T(8,128)(2,1)S(1)}, u32[]{:S(2)}, u32[]{:S(2)}) async-start(bf16[32,16,1024]{2,1,0:T(8,128)(2,1)} %bitcast.3), calls=%async_computation.2 | async-start | bytes 2097152 | tf_op jit(solution)/shard_map/all_to_all | solution.py:149
  378.4 51.4 %copy-start.28 = (bf16[256,64]{0,1:T(8,128)(2,1)S(1)}, bf16[256,64]{0,1:T(8,128)(2,1)}, u32[]{:S(2)}) copy-start(bf16[256,64]{0,1:T(8,128)(2,1)} %copy-done.27) | copy-start | bytes 98308
  378.4 51.4 %copy-start.40 = (bf16[256,64]{0,1:T(8,128)(2,1)S(1)}, bf16[256,64]{0,1:T(8,128)(2,1)}, u32[]{:S(2)}) copy-start(bf16[256,64]{0,1:T(8,128)(2,1)} %copy-done.39) | copy-start | bytes 98308
  378.4 50.1 %all-to-all-start.3 = ((bf16[32,16,1024]{2,1,0:T(8,128)(2,1)}), bf16[32,16,1024]{2,1,0:T(8,128)(2,1)S(1)}, u32[]{:S(2)}, u32[]{:S(2)}) async-start(bf16[32,16,1024]{2,1,0:T(8,128)(2,1)} %stack.5), calls=%async_computation.3 | async-start | bytes 2097152 | tf_op jit(solution)/shard_map/all_to_all | solution.py:126
  428.5 1.3 copy-start.23
  428.6 1.3 copy-start.38
  430.0 0.8 copy-start.21
  430.0 0.8 copy-start.36
  431.3 1.0 copy-start.6
  431.4 1.0 copy-start.19
  431.4 1.0 copy-start.34
  432.9 1.0 copy-start.7
  432.9 1.0 copy-start.17
  432.9 1.0 copy-start.32
  434.4 1.0 copy-start.8
  434.5 1.0 copy-start.15
  434.5 1.0 copy-start.30
  436.0 1.0 copy-start.9
  437.5 1.0 copy-start.10
  440.5 1.0 copy-start.11
  448.0 18.3 %all-to-all-start.4 = ((bf16[16,16,1024]{2,1,0:T(8,128)(2,1)}), bf16[16,16,1024]{2,1,0:T(8,128)(2,1)S(1)}, u32[]{:S(2)}, u32[]{:S(2)}) async-start(bf16[16,16,1024]{2,1,0:T(8,128)(2,1)} %bitcast.5), calls=%async_computation.4 | async-start | bytes 1048576 | tf_op jit(solution)/shard_map/all_to_all | solution.py:145
  454.8 48.6 %copy-start.26 = (bf16[16,1024]{1,0:T(8,128)(2,1)S(1)}, bf16[16,1024]{1,0:T(8,128)(2,1)}, u32[]{:S(2)}) copy-start(bf16[16,1024]{1,0:T(8,128)(2,1)} %param.36) | copy-start | bytes 98308
  466.3 36.9 %all-to-all-start.5 = ((bf16[32,16,1024]{2,1,0:T(8,128)(2,1)}), bf16[32,16,1024]{2,1,0:T(8,128)(2,1)S(1)}, u32[]{:S(2)}, u32[]{:S(2)}) async-start(bf16[32,16,1024]{2,1,0:T(8,128)(2,1)} %bitcast.6), calls=%async_computation.5 | async-start | bytes 2097152 | tf_op jit(solution)/shard_map/all_to_all | solution.py:149
